TPU v7x, 32 devices: a whole 2x2x4 slice. The times are simulated.
32 devices in a mesh: rows: 8 (over z, y), grp: 4 (over x, core).
Axes of the slice: x: 2, y: 2, z: 4, core: 2. Of those that a mesh axis runs over, the one named last changes fastest.
Arguments:
- features: bfloat16 [4096, 512], P(('rows', 'grp')), may hold values from -6 to 6
- tile_entries: bfloat16 [64, 64, 1024], P(('rows', 'grp'))
- tile_columns: int32 [64, 16], P(('rows', 'grp')), may hold values from 0 to 63, as said below
- tiles_per_row: int32 [64], P(('rows', 'grp')), may hold values from 1 to 16, as said below
- rev_vals: bfloat16 [64, 64, 1024], P(('rows', 'grp'))
- rev_cols: int32 [64, 16], P(('rows', 'grp')), may hold values from 0 to 63, as said below
- rev_count: int32 [64], P(('rows', 'grp')), may hold values from 1 to 16, as said below
- w_first: bfloat16 [512, 512], replicated, may hold values from -0.25 to 0.25
- w_second: bfloat16 [512, 512], replicated, may hold values from -0.25 to 0.25
- cotangent: bfloat16 [4096, 512], P(('rows', 'grp')), may hold values from -0.09375 to 0.09375
Outputs:
- z_out: bfloat16 [4096, 512], P(('rows', 'grp'))
- grad_first: float32 [512, 512], replicated
- grad_second: float32 [512, 512], replicated
Inputs may be any that keep to these rules, and one draw needn't show every extreme that they name: `tile_columns`: within each block row the 16 slots name distinct block columns; for each slot s, the block columns named in slot s over all block rows are all different. `tiles_per_row`: some block row has exactly 16 tiles. `rev_cols`: within each block column the slots name distinct block rows; the live transposed slots of block column c hold exactly the transposes of the live tiles of A in block column c. `rev_count`: some block column has exactly 16 tiles.
All inputs are finite; a program needn't handle non-finite values.
Results may differ from a plain program's by a relative error of at most 0.0062.
Values may be sent and summed in bfloat16 or wider, within the bound.
No kernel may reach another device: no remote copies, remote signals or barrier semaphores. Data moves between devices by JAX's collectives and lax.ppermute only.
A program may use at most 128 MiB of HBM per device.

v0:
```python
import jax
import jax.numpy as jnp
from jax import lax
from jax.sharding import PartitionSpec as P


def active_mask(columns, counts):
    return lax.broadcasted_iota(jnp.int32, columns.shape, 1) < counts[:, None]


def aggregate(panel_vals, strip_columns, strip_count, everyone, own_rows):
    blocks, size_block, span_width = panel_vals.shape
    slot_count = span_width // size_block
    channels = everyone.shape[1]
    block_table = everyone.reshape(-1, size_block, channels)
    weights = active_mask(strip_columns, strip_count).astype(everyone.dtype)
    picked = (block_table[strip_columns] * weights[:, :, None, None]).reshape(
        blocks, slot_count * size_block, channels
    )
    summed_rows = jnp.einsum("bik,bkc->bic", panel_vals, picked, preferred_element_type=jnp.float32)
    return summed_rows.reshape(blocks * size_block, channels) + own_rows.astype(jnp.float32)


def spread_terms(panel_vals, strip_columns, strip_count, grad_rows):
    blocks, size_block, span_width = panel_vals.shape
    slot_count = span_width // size_block
    channels = grad_rows.shape[1]
    products = jnp.einsum(
        "bik,bic->bkc",
        panel_vals,
        grad_rows.reshape(blocks, size_block, channels),
        preferred_element_type=jnp.float32,
    )
    products = products.reshape(blocks * slot_count, size_block, channels)
    targets = strip_columns.reshape(-1)
    slot_active = active_mask(strip_columns, strip_count).reshape(-1)

    def term_rows(first_row, row_count):
        segment_ids = row_count // size_block
        slot_offset = targets - first_row // size_block
        inside_bound = slot_active & (slot_offset >= 0) & (slot_offset < segment_ids)
        labels = jnp.where(inside_bound, slot_offset, segment_ids)
        summed_rows = jax.ops.segment_sum(products, labels, num_segments=segment_ids + 1)
        return summed_rows[:segment_ids].reshape(row_count, channels)

    return term_rows


def silu_slope(values):
    sigmoid_part = jax.nn.sigmoid(values)
    return sigmoid_part * (1.0 + values * (1.0 - sigmoid_part))


def to_columns(row_block):
    return lax.all_to_all(row_block, "grp", split_axis=1, concat_axis=0, tiled=True)


def mix_columns(column_block, panel_vals, strip_columns, strip_count):
    everyone = lax.all_gather(column_block, "rows", axis=0, tiled=True)
    return aggregate(panel_vals, strip_columns, strip_count, everyone, column_block)


def shards(
    features,
    tile_entries,
    tile_columns,
    tiles_per_row,
    rev_vals,
    rev_cols,
    rev_count,
    w_first,
    w_second,
    cotangent,
):
    panel_vals, strip_columns, strip_count = (
        lax.all_gather(tile_entries, "grp", axis=0, tiled=True),
        lax.all_gather(tile_columns, "grp", axis=0, tiled=True),
        lax.all_gather(tiles_per_row, "grp", axis=0, tiled=True),
    )

    def propagate(row_block):
        column_block = to_columns(row_block)
        summed_rows = mix_columns(column_block, panel_vals, strip_columns, strip_count).astype(
            jnp.bfloat16
        )
        return lax.all_to_all(summed_rows, "grp", split_axis=0, concat_axis=1, tiled=True)

    mixed_first = propagate(features)
    pre_first = jnp.dot(mixed_first, w_first, preferred_element_type=jnp.float32)
    hidden = jax.nn.silu(pre_first).astype(jnp.bfloat16)
    mixed_second = propagate(hidden)
    z_out = jnp.dot(mixed_second, w_second, preferred_element_type=jnp.float32).astype(jnp.bfloat16)
    local_second = jnp.einsum(
        "nh,nk->hk", mixed_second, cotangent, preferred_element_type=jnp.float32
    )
    grad_second = lax.psum(local_second, ("rows", "grp"))
    back_second = jnp.dot(cotangent, w_second.T, preferred_element_type=jnp.float32).astype(
        jnp.bfloat16
    )
    column_block = to_columns(back_second)
    term_rows = spread_terms(panel_vals, strip_columns, strip_count, column_block)
    summed_rows = lax.psum_scatter(
        term_rows(jnp.int32(0), column_block.shape[0] * lax.axis_size("rows")),
        "rows",
        scatter_dimension=0,
        tiled=True,
    )
    summed_rows = summed_rows + column_block.astype(jnp.float32)
    back_hidden = lax.all_to_all(summed_rows, "grp", split_axis=0, concat_axis=1, tiled=True)
    back_first = (back_hidden * silu_slope(pre_first)).astype(jnp.bfloat16)
    local_first = jnp.einsum(
        "nh,nk->hk", mixed_first, back_first, preferred_element_type=jnp.float32
    )
    grad_first = lax.psum(local_first, ("rows", "grp"))
    return (z_out, grad_first, grad_second)


def solution(mesh):
    placed = (
        P(("rows", "grp"), None),
        P(("rows", "grp"), None, None),
        P(("rows", "grp"), None),
        P(("rows", "grp")),
        P(("rows", "grp"), None, None),
        P(("rows", "grp"), None),
        P(("rows", "grp")),
        P(),
        P(),
        P(("rows", "grp"), None),
    )
    return jax.shard_map(
        shards,
        mesh=mesh,
        in_specs=placed,
        out_specs=(P(("rows", "grp"), None), P(), P()),
        check_vma=False,
    )
```

profile of v0, /device:TPU:0, one launch (start us, length us, event | category | flops | bytes accessed | tf_op | source)
XLA Modules:
  0.0 358.8 jit_solution(1867615093499603882)
XLA Ops:
  8.3 8.6 %all_to_all.105 = bf16[128,4,128]{0,2,1:T(8,128)(2,1)S(1)} all-to-all(bf16[128,4,128]{0,2,1:T(8,128)(2,1)S(1)} %bitcast.96), channel_id=1, replica_groups=mesh['rows'=8,'grp'=4] {'grp'}, dimensions={1} | all-to-all | bytes 262144 | tf_op jit(solution)/shard_map/all_to_all | solution.py:55
  21.3 4.3 %all-reduce = s32[8]{0:T(128)S(1)} all-reduce(s32[8]{0:T(128)S(1)} %dynamic-update-slice), channel_id=1, replica_groups=mesh['rows'=8,'grp'=4] {'grp'}, use_global_device_ids=true, to_apply=%add | all-reduce | flops 8 | bytes 64
  25.6 5.3 %all-gather = s32[4,2,16]{2,1,0:T(2,128)S(1)} all-gather(s32[1,2,16]{2,1,0:T(2,128)} %bitcast.98), channel_id=1, replica_groups=mesh['rows'=8,'grp'=4] {'grp'}, dimensions={0}, use_global_device_ids=true | all-gather | bytes 640 | tf_op jit(solution)/shard_map/all_gather | solution.py:77
  31.2 27.2 %all-gather.5.cloned.1.call-done = bf16[4096,128]{1,0:T(8,128)(2,1)} async-done(((bf16[512,128]{1,0:T(8,128)(2,1)}), bf16[4096,128]{1,0:T(8,128)(2,1)}) %all-gather.5.cloned.1.call-update) | async-done | bytes 1048592 | tf_op jit(solution)/shard_map/all_gather | solution.py:59
  58.4 2.2 gather_fusion
  60.6 2.2 bitcast_multiply_fusion.1
  62.8 12.7 %all-gather.7.cloned.1.call-done = bf16[8,64,1024]{2,1,0:T(8,128)(2,1)} async-done(((bf16[2,64,1024]{2,1,0:T(8,128)(2,1)}), bf16[8,64,1024]{2,1,0:T(8,128)(2,1)}) %all-gather.7.cloned.1.call-update) | async-done | bytes 1048592 | tf_op jit(solution)/shard_map/all_gather | solution.py:76
  75.5 2.4 fusion.11
  78.1 7.2 %all_to_all.106 = bf16[4,128,128]{1,2,0:T(8,128)(2,1)S(1)} all-to-all(bf16[4,128,128]{1,2,0:T(8,128)(2,1)S(1)} %add_convert_fusion.1), channel_id=1, replica_groups=mesh['rows'=8,'grp'=4] {'grp'}, dimensions={0} | all-to-all | bytes 262144 | tf_op jit(solution)/shard_map/all_to_all | solution.py:86
  85.6 7.7 %all_to_all.107 = bf16[128,4,128]{2,0,1:T(8,128)(2,1)} all-to-all(bf16[128,4,128]{2,0,1:T(8,128)(2,1)S(1)} %copy_bitcast_fusion.1), channel_id=1, replica_groups=mesh['rows'=8,'grp'=4] {'grp'}, dimensions={1} | all-to-all | bytes 262144 | tf_op jit(solution)/shard_map/all_to_all | solution.py:55
  94.3 3.3 all-to-all-start.4
  97.9 4.4 %all-to-all-done.4 = bf16[128,4,128]{2,0,1:T(8,128)(2,1)S(1)} async-done(((bf16[128,4,128]{2,0,1:T(8,128)(2,1)}), bf16[128,4,128]{2,0,1:T(8,128)(2,1)S(1)}, u32[]{:S(2)}, u32[]{:S(2)}) %all-to-all-start.4) | async-done | bytes 131104 | tf_op jit(solution)/shard_map/all_to_all | solution.py:55
  102.3 2.7 convolution_bitcast_fusion
  105.0 5.4 %copy.39 = f32[8,1024,128]{2,1,0:T(8,128)} copy(f32[8,1024,128]{1,2,0:T(8,128)} %convolution_bitcast_fusion) | data formatting | bytes 8388608 | tf_op jit(solution)/shard_map/bik,bic->bkc/dot_general | solution.py:28
  110.6 13.6 %scatter_fusion = f32[65,64,128]{2,1,0:T(8,128)S(1)} fusion(f32[65,64,128]{2,1,0:T(8,128)S(1)} %broadcast_in_dim.6, s32[128]{0:T(128)S(1)} %fusion.6, f32[128,64,128]{2,1,0:T(8,128)} %bitcast.79), kind=kCustom, calls=%fused_computation.2 | custom fusion | flops 1048576 | bytes 12583424 | tf_op jit(solution)/shard_map/scatter-add | solution.py:43
  125.7 7.9 %all-gather.9.cloned.1.call-done = bf16[4096,128]{1,0:T(8,128)(2,1)} async-done(((bf16[512,128]{1,0:T(8,128)(2,1)}), bf16[4096,128]{1,0:T(8,128)(2,1)}) %all-gather.9.cloned.1.call-update) | async-done | bytes 1048592 | tf_op jit(solution)/shard_map/all_gather | solution.py:59
  133.6 2.2 gather_fusion.1
  138.4 7.2 %all_to_all.108 = bf16[4,128,128]{2,1,0:T(8,128)(2,1)S(1)} all-to-all(bf16[4,128,128]{2,1,0:T(8,128)(2,1)S(1)} %add_convert_fusion), channel_id=1, replica_groups=mesh['rows'=8,'grp'=4] {'grp'}, dimensions={0} | all-to-all | bytes 262144 | tf_op jit(solution)/shard_map/all_to_all | solution.py:86
  145.7 58.0 %reduce-scatter.2.cloned.1.call-done = f32[512,128]{1,0:T(8,128)} async-done(((f32[4096,128]{1,0:T(8,128)}), f32[512,128]{1,0:T(8,128)}) %reduce-scatter.2.cloned.1.call-update) | async-done | bytes 262160 | tf_op jit(solution)/shard_map/reduce_scatter | solution.py:102
  203.7 1.7 convert_add_fusion
  205.4 3.4 all-to-all-start.5
  210.1 4.7 %all-to-all-done.5 = f32[4,128,128]{2,1,0:T(8,128)S(1)} async-done(((f32[4,128,128]{2,1,0:T(8,128)}), f32[4,128,128]{2,1,0:T(8,128)S(1)}, u32[]{:S(2)}, u32[]{:S(2)}) %all-to-all-start.5) | async-done | bytes 262176 | tf_op jit(solution)/shard_map/all_to_all | solution.py:109
  217.0 131.9 %all-reduce.4.cloned.1.call-done = (f32[512,512]{1,0:T(8,128)}, f32[512,512]{1,0:T(8,128)}) async-done(((f32[512,512]{1,0:T(8,128)}, f32[512,512]{1,0:T(8,128)}), (f32[512,512]{1,0:T(8,128)}, f32[512,512]{1,0:T(8,128)})) %all-reduce.4.cloned.1.call-update) | async-done | bytes 2097168 | tf_op jit(solution)/shard_map/psum | solution.py:114
  348.9 2.4 copy.53
  (54 shorter events, 15.8 us)
Async XLA Ops:
  7.2 86.1 %copy-start = (bf16[512,512]{1,0:T(8,128)(2,1)S(1)}, bf16[512,512]{1,0:T(8,128)(2,1)}, u32[]{:S(2)}) copy-start(bf16[512,512]{1,0:T(8,128)(2,1)} %param.15) | copy-start | bytes 1572868
  7.2 51.3 %all-gather.5.cloned.1.call-start = ((), (), s32[]{:S(2)}) async-start(), calls=%async_computation.7 | async-start | bytes 1179648 | tf_op jit(solution)/shard_map/all_gather | solution.py:59
  17.7 57.8 %all-gather.7.cloned.1.call-start = ((), (), s32[]{:S(2)}) async-start(), calls=%async_computation.8 | async-start | bytes 1310720 | tf_op jit(solution)/shard_map/all_gather | solution.py:76
  18.5 115.1 %all-gather.9.cloned.1.call-start = ((), (), s32[]{:S(2)}) async-start(), calls=%async_computation.9 | async-start | bytes 1179648 | tf_op jit(solution)/shard_map/all_gather | solution.py:59
  62.8 22.4 %copy-start.5 = (bf16[512,512]{1,0:T(8,128)(2,1)S(1)}, bf16[512,512]{1,0:T(8,128)(2,1)}, u32[]{:S(2)}) copy-start(bf16[512,512]{1,0:T(8,128)(2,1)} %param.14) | copy-start | bytes 1572868
  77.9 15.4 %copy-start.6 = (bf16[128,512]{1,0:T(8,128)(2,1)S(1)}, bf16[128,512]{1,0:T(8,128)(2,1)}, u32[]{:S(2)}) copy-start(bf16[128,512]{1,0:T(8,128)(2,1)} %param.16) | copy-start | bytes 393220
  77.9 24.3 %copy-start.1 = (bf16[8,64,1024]{2,1,0:T(8,128)(2,1)S(1)}, bf16[8,64,1024]{2,1,0:T(8,128)(2,1)}, u32[]{:S(2)}) copy-start(bf16[8,64,1024]{2,1,0:T(8,128)(2,1)} %all-gather.7.cloned.1.call-done) | copy-start | bytes 3145732
  94.3 7.9 %all-to-all-start.4 = ((bf16[128,4,128]{2,0,1:T(8,128)(2,1)}), bf16[128,4,128]{2,0,1:T(8,128)(2,1)S(1)}, u32[]{:S(2)}, u32[]{:S(2)}) async-start(bf16[128,4,128]{2,0,1:T(8,128)(2,1)} %bitcast.76), calls=%async_computation.4 | async-start | bytes 262144 | tf_op jit(solution)/shard_map/all_to_all | solution.py:55
  97.7 106.0 %reduce-scatter.2.cloned.1.call-start = ((), (), s32[]{:S(2)}) async-start(), calls=%async_computation.10 | async-start | bytes 2359296 | tf_op jit(solution)/shard_map/reduce_scatter | solution.py:102
  135.8 1.6 copy-start.2
  137.4 0.9 copy-start.3
  205.4 9.4 %all-to-all-start.5 = ((f32[4,128,128]{2,1,0:T(8,128)}), f32[4,128,128]{2,1,0:T(8,128)S(1)}, u32[]{:S(2)}, u32[]{:S(2)}) async-start(f32[4,128,128]{2,1,0:T(8,128)} %bitcast.28), calls=%async_computation.6 | async-start | bytes 524288 | tf_op jit(solution)/shard_map/all_to_all | solution.py:109
  208.8 140.1 %all-reduce.4.cloned.1.call-start = ((), (), s32[]{:S(2)}) async-start(), calls=%async_computation.11 | async-start | bytes 4194304 | tf_op jit(solution)/shard_map/psum | solution.py:114
  348.9 2.4 copy-start.4
Sparse Core Ops, SparseCore 0:
  17.9 40.5 all-gather.4
  60.0 15.4 all-gather.6
  93.4 40.1 all-gather.8
  137.0 66.6 reduce-scatter.1
  216.3 132.6 all-reduce.3
where the time goes:
time: 360 us; the launch traced here: 359 us
  waiting for transfers between devices  247 us (69%)
  blocking collectives  40.2 us (11%)
  local copies, waits for them, and re-layouts  20.5 us (6%)
  other arithmetic  19.3 us (5%)
  between operations  14.7 us (4%)
  matrix products  9.67 us (3%)
  starting transfers between devices  6.93 us (2%)
    psum x1, waiting for transfers between devices, shards(): grad_first = lax.psum(local_first, ('rows', 'grp'))  132 us
    reduce_scatter x1, waiting for transfers between devices, shards(): lax.psum_scatter(term_rows(jnp.int32(0), column_block.shape[0] * lax.axis...  58 us
    all_gather x2, waiting for transfers between devices, mix_columns(): everyone = lax.all_gather(column_block, 'rows', axis=0, tiled=True)  35.2 us
    all_to_all x2, blocking collectives, to_columns(): lax.all_to_all(row_block, 'grp', split_axis=1, concat_axis=0, tiled=True)  16.3 us
    all_to_all x2, blocking collectives, propagate(): lax.all_to_all(summed_rows, 'grp', split_axis=0, concat_axis=1, tiled=True)  14.3 us
    scatter-add x1, other arithmetic, term_rows(): jax.ops.segment_sum(products, labels, num_segments=segment_ids + 1)  13.6 us
    all_gather x1, waiting for transfers between devices, shards(): lax.all_gather(tile_entries, 'grp', axis=0, tiled=True)  12.7 us
  transfers between devices with their start and end apart: 7, of which 7 were waited for; matrix products, arithmetic and copies ran while one was open for 11% of the time, Pallas kernels for 0%

commit v1 on v0

--- a/solution.py
+++ b/solution.py
@@ -111,7 +111,7 @@
     local_first = jnp.einsum(
         "nh,nk->hk", mixed_first, back_first, preferred_element_type=jnp.float32
     )
-    grad_first = lax.psum(local_first, ("rows", "grp"))
+    grad_first = jnp.sum(lax.all_gather(local_first, ("rows", "grp")), axis=0)
     return (z_out, grad_first, grad_second)
 
 

time: 360 us -> 523 us (1.45)
  waiting for transfers between devices: 247 us -> 390 us
  other arithmetic: 19.3 us -> 33.2 us
  blocking collectives: 40.2 us -> 50.2 us
    all_gather x0 -> x1, waiting for transfers between devices: none -> 180 us  [shards(): grad_first = jnp.sum(lax.all_gather(local_first, ('rows', 'grp')), axis=0)]
    reduce_sum x0 -> x1, other arithmetic: none -> 13.3 us  [shards(): grad_first = jnp.sum(lax.all_gather(local_first, ('rows', 'grp')), axis=0)]
    all_gather x1, waiting for transfers between devices: 12.7 us -> 0.02 us  [shards(): lax.all_gather(tile_entries, 'grp', axis=0, tiled=True)]
    psum x1, waiting for transfers between devices: 132 us -> 120 us  [shards(): grad_second = lax.psum(local_second, ('rows', 'grp'))]
    reduce_scatter x1, waiting for transfers between devices: 58 us -> 48 us  [shards(): lax.psum_scatter(term_rows(jnp.int32(0), column_block.shape[0] * lax.axis...]
    all_to_all x0 -> x1, blocking collectives: none -> 8.58 us  [shards(): lax.all_to_all(summed_rows, 'grp', split_axis=0, concat_axis=1, tiled=True)]
    all_gather x2, waiting for transfers between devices: 35.2 us -> 41.3 us  [mix_columns(): everyone = lax.all_gather(column_block, 'rows', axis=0, tiled=True)]
  transfers between devices with their start and end apart: 7 -> 7, of which waited for: 7 -> 5; matrix products, arithmetic and copies ran while one was open for 11% -> 12% of each run, Pallas kernels for 0% -> 0%
where the time goes in v1:
time: 523 us; the launch traced here: 522 us
  waiting for transfers between devices  390 us (75%)
  blocking collectives  50.2 us (10%)
  other arithmetic  33.2 us (6%)
  local copies, waits for them, and re-layouts  20.5 us (4%)
  between operations  15 us (3%)
  matrix products  9.93 us (2%)
    all_gather x1, waiting for transfers between devices, shards(): grad_first = jnp.sum(lax.all_gather(local_first, ('rows', 'grp')), axis=0)  180 us
    psum x1, waiting for transfers between devices, shards(): grad_second = lax.psum(local_second, ('rows', 'grp'))  120 us
    reduce_scatter x1, waiting for transfers between devices, shards(): lax.psum_scatter(term_rows(jnp.int32(0), column_block.shape[0] * lax.axis...  48 us
    all_gather x2, waiting for transfers between devices, mix_columns(): everyone = lax.all_gather(column_block, 'rows', axis=0, tiled=True)  41.3 us
    all_to_all x2, blocking collectives, to_columns(): lax.all_to_all(row_block, 'grp', split_axis=1, concat_axis=0, tiled=True)  16.3 us
    all_to_all x2, blocking collectives, propagate(): lax.all_to_all(summed_rows, 'grp', split_axis=0, concat_axis=1, tiled=True)  14.9 us
    scatter-add x1, other arithmetic, term_rows(): jax.ops.segment_sum(products, labels, num_segments=segment_ids + 1)  13.6 us
    reduce_sum x1, other arithmetic, shards(): grad_first = jnp.sum(lax.all_gather(local_first, ('rows', 'grp')), axis=0)  13.3 us
  transfers between devices with their start and end apart: 7, of which 5 were waited for; matrix products, arithmetic and copies ran while one was open for 12% of the time, Pallas kernels for 0%

profile of v1, /device:TPU:0, one launch (start us, length us, event | category | flops | bytes accessed | tf_op | source)
XLA Modules:
  0.0 522.2 jit_solution(15022331372317094167)
XLA Ops:
  9.0 8.6 %all_to_all.105 = bf16[128,4,128]{0,2,1:T(8,128)(2,1)S(1)} all-to-all(bf16[128,4,128]{0,2,1:T(8,128)(2,1)S(1)} %bitcast.99), channel_id=1, replica_groups=mesh['rows'=8,'grp'=4] {'grp'}, dimensions={1} | all-to-all | bytes 262144 | tf_op jit(solution)/shard_map/all_to_all | solution.py:55
  21.9 3.3 all-to-all-start.4
  25.3 5.4 %all-reduce = s32[8]{0:T(128)S(1)} all-reduce(s32[8]{0:T(128)S(1)} %dynamic-update-slice), channel_id=1, replica_groups=mesh['rows'=8,'grp'=4] {'grp'}, use_global_device_ids=true, to_apply=%add | all-reduce | flops 8 | bytes 64
  30.6 5.1 all-gather.1
  36.0 3.9 convolution_bitcast_fusion
  39.9 5.4 %copy.39 = f32[8,1024,128]{2,1,0:T(8,128)} copy(f32[8,1024,128]{1,2,0:T(8,128)} %convolution_bitcast_fusion) | data formatting | bytes 8388608 | tf_op jit(solution)/shard_map/bik,bic->bkc/dot_general | solution.py:28
  45.5 13.6 %scatter_fusion = f32[65,64,128]{2,1,0:T(8,128)S(1)} fusion(f32[65,64,128]{2,1,0:T(8,128)S(1)} %broadcast_in_dim.6, s32[128]{0:T(128)S(1)} %fusion.6, f32[128,64,128]{2,1,0:T(8,128)} %bitcast.81), kind=kCustom, calls=%fused_computation.2 | custom fusion | flops 1048576 | bytes 12583424 | tf_op jit(solution)/shard_map/scatter-add | solution.py:43
  59.1 1.5 slice.8
  61.0 11.0 %all-gather.7.cloned.1.call-done = bf16[4096,128]{1,0:T(8,128)(2,1)} async-done(((bf16[512,128]{1,0:T(8,128)(2,1)}), bf16[4096,128]{1,0:T(8,128)(2,1)}) %all-gather.7.cloned.1.call-update) | async-done | bytes 1048592 | tf_op jit(solution)/shard_map/all_gather | solution.py:59
  71.9 3.4 gather_fusion
  75.3 2.6 bitcast_multiply_fusion.1
  78.6 7.2 %all_to_all.106 = bf16[4,128,128]{1,2,0:T(8,128)(2,1)S(1)} all-to-all(bf16[4,128,128]{1,2,0:T(8,128)(2,1)S(1)} %add_convert_fusion.1), channel_id=1, replica_groups=mesh['rows'=8,'grp'=4] {'grp'}, dimensions={0} | all-to-all | bytes 262144 | tf_op jit(solution)/shard_map/all_to_all | solution.py:86
  86.1 7.7 %all_to_all.107 = bf16[128,4,128]{2,0,1:T(8,128)(2,1)} all-to-all(bf16[128,4,128]{2,0,1:T(8,128)(2,1)S(1)} %copy_bitcast_fusion.1), channel_id=1, replica_groups=mesh['rows'=8,'grp'=4] {'grp'}, dimensions={1} | all-to-all | bytes 262144 | tf_op jit(solution)/shard_map/all_to_all | solution.py:55
  93.9 48.0 %reduce-scatter.2.cloned.1.call-done = f32[512,128]{1,0:T(8,128)} async-done(((f32[4096,128]{1,0:T(8,128)}), f32[512,128]{1,0:T(8,128)}) %reduce-scatter.2.cloned.1.call-update) | async-done | bytes 262160 | tf_op jit(solution)/shard_map/reduce_scatter | solution.py:102
  142.8 8.6 %all_to_all.108 = f32[4,128,128]{2,1,0:T(8,128)S(1)} all-to-all(f32[4,128,128]{2,1,0:T(8,128)S(1)} %bitcast.94), channel_id=1, replica_groups=mesh['rows'=8,'grp'=4] {'grp'}, dimensions={0} | all-to-all | bytes 524288 | tf_op jit(solution)/shard_map/all_to_all | solution.py:109
  151.4 1.3 fusion.2
  152.8 30.3 %all-gather.11.cloned.1.call-done = bf16[4096,128]{1,0:T(8,128)(2,1)} async-done(((bf16[512,128]{1,0:T(8,128)(2,1)}), bf16[4096,128]{1,0:T(8,128)(2,1)}) %all-gather.11.cloned.1.call-update) | async-done | bytes 1048592 | tf_op jit(solution)/shard_map/all_gather | solution.py:59
  183.2 3.4 gather_fusion.1
  186.5 2.5 bitcast_multiply_fusion
  189.9 7.7 %all_to_all.109 = bf16[4,128,128]{2,1,0:T(8,128)(2,1)S(1)} all-to-all(bf16[4,128,128]{2,1,0:T(8,128)(2,1)S(1)} %add_convert_fusion), channel_id=1, replica_groups=mesh['rows'=8,'grp'=4] {'grp'}, dimensions={0} | all-to-all | bytes 262144 | tf_op jit(solution)/shard_map/all_to_all | solution.py:86
  200.0 180.0 %all-gather.13.cloned.1.call-done = f32[16384,512]{1,0:T(8,128)} async-done(((f32[512,512]{1,0:T(8,128)}), f32[16384,512]{1,0:T(8,128)}) %all-gather.13.cloned.1.call-update) | async-done | bytes 33554448 | tf_op jit(solution)/shard_map/all_gather | solution.py:114
  380.0 13.3 %reduce_sum.9 = f32[512,512]{1,0:T(8,128)} reduce(f32[32,512,512]{2,1,0:T(8,128)} %bitcast.80, f32[]{:T(128)} %constant.26.clone.1), dimensions={0}, to_apply=%region_2.3 | reduce | flops 8126464 | bytes 34603012 | tf_op jit(solution)/shard_map/reduce_sum | solution.py:114
  393.3 119.8 %all-reduce.3.cloned.1.call-done = f32[512,512]{1,0:T(8,128)} async-done(((f32[512,512]{1,0:T(8,128)}), f32[512,512]{1,0:T(8,128)}) %all-reduce.3.cloned.1.call-update) | async-done | bytes 1048592 | tf_op jit(solution)/shard_map/psum | solution.py:96
  513.1 2.3 copy.52
  (58 shorter events, 11.6 us)
Async XLA Ops:
  7.2 11.3 %copy-start = (bf16[512,512]{1,0:T(8,128)(2,1)S(1)}, bf16[512,512]{1,0:T(8,128)(2,1)}, u32[]{:S(2)}) copy-start(bf16[512,512]{1,0:T(8,128)(2,1)} %param.15) | copy-start | bytes 1572868
  7.2 13.2 %copy-start.7 = (u32[32]{0:T(128)S(1)}, u32[32]{0:T(128)}, u32[]{:S(2)}) copy-start(u32[32]{0:T(128)} %constant.32) | copy-start | bytes 388
  7.2 14.4 %copy-start.6 = (s32[2]{0:T(128)S(1)}, s32[2]{0:T(128)}, u32[]{:S(2)}) copy-start(s32[2]{0:T(128)} %param.13) | copy-start | bytes 28
  7.2 23.4 %copy-start.5 = (s32[2,16]{1,0:T(2,128)S(1)}, s32[2,16]{1,0:T(2,128)}, u32[]{:S(2)}) copy-start(s32[2,16]{1,0:T(2,128)} %param.12) | copy-start | bytes 388
  7.2 28.8 %all-gather.9.cloned.1.call-start = ((), (), s32[]{:S(2)}) async-start(), calls=%async_computation.8 | async-start | bytes 1310720 | tf_op jit(solution)/shard_map/all_gather | solution.py:76
  7.9 64.0 %all-gather.7.cloned.1.call-start = ((), (), s32[]{:S(2)}) async-start(), calls=%async_computation.7 | async-start | bytes 1179648 | tf_op jit(solution)/shard_map/all_gather | solution.py:59
  21.9 14.1 %all-to-all-start.4 = ((bf16[128,4,128]{2,0,1:T(8,128)(2,1)}), bf16[128,4,128]{2,0,1:T(8,128)(2,1)S(1)}, u32[]{:S(2)}, u32[]{:S(2)}) async-start(bf16[128,4,128]{2,0,1:T(8,128)(2,1)} %bitcast.77), calls=%async_computation.4 | async-start | bytes 262144 | tf_op jit(solution)/shard_map/all_to_all | solution.py:55
  25.2 116.6 %reduce-scatter.2.cloned.1.call-start = ((), (), s32[]{:S(2)}) async-start(), calls=%async_computation.10 | async-start | bytes 2359296 | tf_op jit(solution)/shard_map/reduce_scatter | solution.py:102
  60.6 122.5 %all-gather.11.cloned.1.call-start = ((), (), s32[]{:S(2)}) async-start(), calls=%async_computation.9 | async-start | bytes 1179648 | tf_op jit(solution)/shard_map/all_gather | solution.py:59
  75.3 2.6 copy-start.1
  77.9 7.9 %copy-start.3 = (bf16[512,512]{1,0:T(8,128)(2,1)S(1)}, bf16[512,512]{1,0:T(8,128)(2,1)}, u32[]{:S(2)}) copy-start(bf16[512,512]{1,0:T(8,128)(2,1)} %param.14) | copy-start | bytes 1572868
  93.8 286.2 %all-gather.13.cloned.1.call-start = ((), (), s32[]{:S(2)}) async-start(), calls=%async_computation.12 | async-start | bytes 34603008 | tf_op jit(solution)/shard_map/all_gather | solution.py:114
  152.8 360.3 %all-reduce.3.cloned.1.call-start = ((), (), s32[]{:S(2)}) async-start(), calls=%async_computation.11 | async-start | bytes 2097152 | tf_op jit(solution)/shard_map/psum | solution.py:96
  189.0 0.9 copy-start.2
  189.0 8.8 %copy-start.4 = (bf16[128,512]{1,0:T(8,128)(2,1)S(1)}, bf16[128,512]{1,0:T(8,128)(2,1)}, u32[]{:S(2)}) copy-start(bf16[128,512]{1,0:T(8,128)(2,1)} %param.16) | copy-start | bytes 393220
Sparse Core Ops, SparseCore 0:
  9.6 19.4 all-gather.8
  31.8 40.1 all-gather.6
  75.5 66.3 reduce-scatter.1
  143.8 39.2 all-gather.10
  186.4 193.5 all-gather.12
  385.1 127.9 all-reduce.2
